TPU v7x, 256 devices: a whole 4x4x8 slice. The times are simulated.
256 devices in a mesh: row: 32 (over z_lo, x, core), col: 8 (over z_hi, y).
Axes of the slice: x: 4, y: 4, z: 8 (z_hi: 2, z_lo: 4; z = z_hi * 4 + z_lo), core: 2. Of those that a mesh axis runs over, the one named last changes fastest.
Arguments:
- right_sides: float32 [16384, 1024], P('row', 'col'), may hold values from -6 to 6
- pencil_s: float32 [16384, 512], P('row'), as said below
- pencil_t: float32 [16384, 512], P('row'), as said below
- value_alpha: float32 [4096], replicated, may hold values from -3 to -0.5
- value_beta: float32 [4096], replicated, may hold values from 0.5 to 1
- selected: int32 [1024], P('col'), may hold values from 0 to 4095
- block_slot: int32 [64], replicated, may hold values from 0 to 63, as said below
- right_basis: float32 [65536, 2, 256], P('row', None, 'col'), may hold values from -0.25 to 0.25
- vectors: float32 [65536, 1024], P('row', 'col'), may hold values from -6 to 6
Outputs:
- updated_sides: float32 [16384, 1024], P('row', 'col')
- updated_vectors: float32 [65536, 1024], P('row', 'col')
Inputs may be any that keep to these rules, and one draw needn't show every extreme that they name: A permutation: logical block b of 256 rows is stored at slot block_slot[b]. `pencil_s`: in the window, entries left of the diagonal are 0 and diagonal entries lie in [1, 2]. `pencil_t`: in the window, entries left of the diagonal are 0 and diagonal entries lie in [1, 2].
All inputs are finite; a program needn't handle non-finite values.
Results may differ from a plain program's by a relative error of at most 0.0003.
Values sent between devices are 32-bit elements; how exact they have to be, the bound alone decides.
A program may use at most 64 MiB of HBM per device.

v0:
```python
import jax
import jax.numpy as jnp
from jax import lax
from jax.sharding import PartitionSpec as P

BLK = 256
LEAD_DEV = 512
exact_mode = lax.Precision.HIGHEST
sub_rows = 32


def from_root(block, axis, source):
    block = jnp.where(lax.axis_index(axis) == source, block, jnp.zeros_like(block))
    return lax.psum(block, axis)


def table_lookup(selected, table):
    positions = lax.broadcasted_iota(jnp.int32, (table.shape[0], selected.shape[0]), 0)
    return jnp.sum(jnp.where(positions == selected[None, :], table[:, None], 0.0), axis=0)


def shifted_apply(s_cols, t_cols, solved, shift_alpha, shift_beta):
    first_term = jnp.dot(
        s_cols,
        solved * shift_beta[None, :],
        precision=exact_mode,
        preferred_element_type=jnp.float32,
    )
    second_term = jnp.dot(
        t_cols,
        solved * shift_alpha[None, :],
        precision=exact_mode,
        preferred_element_type=jnp.float32,
    )
    return first_term - second_term


def solve_block(s_diag, t_diag, right, shift_alpha, shift_beta):
    size_rows = s_diag.shape[0]
    upper_mask = lax.broadcasted_iota(jnp.int32, s_diag.shape, 0) <= lax.broadcasted_iota(
        jnp.int32, s_diag.shape, 1
    )
    s_upper = jnp.where(upper_mask, s_diag, 0.0)
    t_upper = jnp.where(upper_mask, t_diag, 0.0)
    turn_count = size_rows // sub_rows

    def one_turn(step, carry):
        remaining, solved_all = carry
        first_row = (turn_count - 1 - step) * sub_rows
        s_small = lax.dynamic_slice(s_upper, (first_row, first_row), (sub_rows, sub_rows))
        t_small = lax.dynamic_slice(t_upper, (first_row, first_row), (sub_rows, sub_rows))
        combined = (
            shift_beta[None, None, :] * s_small[:, :, None]
            - shift_alpha[None, None, :] * t_small[:, :, None]
        )
        pending = lax.dynamic_slice_in_dim(remaining, first_row, sub_rows, 0)
        entries = [None] * sub_rows
        for column in reversed(range(sub_rows)):
            entry_value = pending[column] / combined[column, column]
            entries[column] = entry_value
            pending = pending - combined[:, column, :] * entry_value[None, :]
        solved_small = jnp.stack(entries)
        s_cols = lax.dynamic_slice_in_dim(s_upper, first_row, sub_rows, 1)
        t_cols = lax.dynamic_slice_in_dim(t_upper, first_row, sub_rows, 1)
        remaining = remaining - shifted_apply(s_cols, t_cols, solved_small, shift_alpha, shift_beta)
        solved_all = lax.dynamic_update_slice_in_dim(solved_all, solved_small, first_row, 0)
        return (remaining, solved_all)

    _, solved_all = lax.fori_loop(0, turn_count, one_turn, (right, jnp.zeros_like(right)))
    return solved_all


def block_term(basis_cols, solved):
    matched_rows = lax.all_to_all(solved, "col", split_axis=0, concat_axis=1, tiled=True)
    partial_value = jnp.dot(
        basis_cols, matched_rows, precision=exact_mode, preferred_element_type=jnp.float32
    )
    return lax.psum_scatter(partial_value, "col", scatter_dimension=1, tiled=True)


def on_device(
    right_sides,
    pencil_s,
    pencil_t,
    value_alpha,
    value_beta,
    selected,
    block_slot,
    right_basis,
    vectors,
):
    shift_alpha = table_lookup(selected, value_alpha)
    shift_beta = table_lookup(selected, value_beta)
    slot_count = LEAD_DEV // BLK
    local_eigs = right_sides.shape[1]
    block_count = block_slot.shape[0]
    slot_upper = block_slot[block_count - 2]
    slot_lower = block_slot[block_count - 1]
    s_view = pencil_s.reshape(slot_count, BLK, 2 * BLK)
    t_view = pencil_t.reshape(slot_count, BLK, 2 * BLK)
    side_view = right_sides.reshape(slot_count, BLK, local_eigs)

    def pick_slot(view, slot_index):
        return lax.dynamic_index_in_dim(view, slot_index % slot_count, 0, keepdims=False)

    s_lower = pick_slot(s_view, slot_lower)
    t_lower = pick_slot(t_view, slot_lower)
    lower_local = solve_block(
        s_lower[:, BLK:],
        t_lower[:, BLK:],
        pick_slot(side_view, slot_lower),
        shift_alpha,
        shift_beta,
    )
    solved_lower = from_root(lower_local, "row", slot_lower // slot_count)
    s_upper = pick_slot(s_view, slot_upper)
    t_upper = pick_slot(t_view, slot_upper)
    right_upper = pick_slot(side_view, slot_upper) - shifted_apply(
        s_upper[:, BLK:], t_upper[:, BLK:], solved_lower, shift_alpha, shift_beta
    )
    upper_local = solve_block(
        s_upper[:, :BLK], t_upper[:, :BLK], right_upper, shift_alpha, shift_beta
    )
    solved_upper = from_root(upper_local, "row", slot_upper // slot_count)
    window_x = jnp.concatenate([solved_upper, solved_lower], 0)
    updated = right_sides - shifted_apply(pencil_s, pencil_t, window_x, shift_alpha, shift_beta)
    global_slot = lax.axis_index("row") * slot_count + lax.broadcasted_iota(
        jnp.int32, (slot_count,), 0
    )
    updated_view = updated.reshape(slot_count, BLK, local_eigs)
    updated_view = jnp.where(
        (global_slot == slot_upper)[:, None, None], solved_upper[None], updated_view
    )
    updated_view = jnp.where(
        (global_slot == slot_lower)[:, None, None], solved_lower[None], updated_view
    )
    updated_sides = updated_view.reshape(LEAD_DEV, local_eigs)
    updated_vectors = (
        vectors
        + block_term(right_basis[:, 0, :], solved_upper)
        + block_term(right_basis[:, 1, :], solved_lower)
    )
    return (updated_sides, updated_vectors)


def solution(mesh):
    return jax.shard_map(
        on_device,
        mesh=mesh,
        in_specs=(
            P("row", "col"),
            P("row", None),
            P("row", None),
            P(),
            P(),
            P("col"),
            P(),
            P("row", None, "col"),
            P("row", "col"),
        ),
        out_specs=(P("row", "col"), P("row", "col")),
        check_vma=False,
    )
```

profile of v0, /device:TPU:34, one launch (start us, length us, event | category | flops | bytes accessed | tf_op | source)
XLA Modules:
  0.0 969.3 jit_solution(17689833058718998711)
XLA Ops:
  7.2 1.4 fusion.231
  13.2 1.7 constant_dynamic-slice_fusion.2
  15.9 2.2 select_reduce_fusion
  18.1 18.8 %while.30 = (s32[]{:T(128)}, f32[256,128]{1,0:T(8,128)S(1)}, f32[256,128]{1,0:T(8,128)S(1)}, f32[256,256]{0,1:T(8,128)S(1)}, f32[128]{0:T(128)S(1)}, /*index=5*/...) while((s32[]{:T(128)}, f32[256,128]{1,0:T(8,128)S(1)}, ...), condition=%wide.region_3.4_spmd, body=%wide.region_2.3_spmd.sunk | while | flops 25882888 | bytes 2812127 | solution.py:69
  38.7 244.7 %all-reduce.3.cloned.1.call-done = f32[256,128]{1,0:T(8,128)} async-done(((f32[256,128]{1,0:T(8,128)}), f32[256,128]{1,0:T(8,128)}) %all-reduce.3.cloned.1.call-update) | async-done | bytes 131088 | tf_op jit(solution)/shard_map/psum | solution.py:14
  283.3 1.5 fusion.210
  284.8 1.5 fusion.208
  286.4 18.8 %while.31 = (s32[]{:T(128)}, f32[256,128]{1,0:T(8,128)S(1)}, f32[256,128]{1,0:T(8,128)S(1)}, f32[256,256]{0,1:T(8,128)S(1)}, f32[128]{0:T(128)S(1)}, /*index=5*/...) while((s32[]{:T(128)}, f32[256,128]{1,0:T(8,128)S(1)}, ...), condition=%wide.region_6.7_spmd, body=%wide.region_5.6_spmd.sunk | while | flops 25882888 | bytes 2812127 | solution.py:69
  305.2 7.6 all-to-all-start.1
  313.6 10.1 %all-to-all-done.1 = f32[8,32,128]{2,1,0:T(8,128)S(1)} async-done(((f32[8,32,128]{2,1,0:T(8,128)}), f32[8,32,128]{2,1,0:T(8,128)S(1)}, u32[]{:S(2)}, u32[]{:S(2)}) %all-to-all-start.1) | async-done | bytes 131104 | tf_op jit(solution)/shard_map/all_to_all | solution.py:74
  323.7 9.0 convolution_bitcast_fusion
  332.8 241.7 %all-reduce.5.cloned.1.call-done = f32[256,128]{1,0:T(8,128)} async-done(((f32[256,128]{1,0:T(8,128)}), f32[256,128]{1,0:T(8,128)}) %all-reduce.5.cloned.1.call-update) | async-done | bytes 131088 | tf_op jit(solution)/shard_map/psum | solution.py:14
  574.5 18.5 %all_to_all.38 = f32[8,32,128]{2,1,0:T(8,128)S(1)} all-to-all(f32[8,32,128]{2,1,0:T(8,128)} %bitcast.1125), channel_id=1, replica_groups=mesh['row'=32,'col'=8] {'col'}, dimensions={0} | all-to-all | bytes 262144 | tf_op jit(solution)/shard_map/all_to_all | solution.py:74
  593.0 9.0 convolution_bitcast_fusion.1
  603.7 1.3 fusion.229
  605.3 1.7 copy.47
  606.9 1.1 broadcast_in_dim.304
  609.5 1.0 broadcast_in_dim.309
  611.5 1.2 fusion.217
  612.8 2.2 fusion.207
  615.8 161.8 %reduce-scatter.5.cloned.1.call-done = f32[2048,128]{0,1:T(8,128)} async-done(((f32[2048,1024]{0,1:T(8,128)}), f32[2048,128]{0,1:T(8,128)}) %reduce-scatter.5.cloned.1.call-update) | async-done | bytes 1048592 | tf_op jit(solution)/shard_map/reduce_scatter | solution.py:78
  777.7 182.1 %reduce-scatter.3.cloned.1.call-done = f32[2048,128]{0,1:T(8,128)} async-done(((f32[2048,1024]{0,1:T(8,128)}), f32[2048,128]{0,1:T(8,128)}) %reduce-scatter.3.cloned.1.call-update) | async-done | bytes 1048592 | tf_op jit(solution)/shard_map/reduce_scatter | solution.py:78
  959.7 1.7 add_add_fusion
  961.4 1.3 copy.56
  (1173 shorter events, 37.2 us)
Async XLA Ops:
  7.2 276.2 %all-reduce.3.cloned.1.call-start = ((), (), s32[]{:S(2)}) async-start(), calls=%async_computation.4 | async-start | bytes 262144 | tf_op jit(solution)/shard_map/psum | solution.py:14
  14.9 1.0 copy-start.4
  14.9 1.0 copy-start.7
  14.9 1.0 copy-start.8
  14.9 1.0 copy-start.9
  286.4 37.3 %copy-start.6 = (f32[2048,2,32]{0,2,1:T(8,128)S(1)}, f32[2048,2,32]{0,2,1:T(8,128)}, u32[]{:S(2)}) copy-start(f32[2048,2,32]{0,2,1:T(8,128)} %param.20) | copy-start | bytes 1572868
  305.2 18.5 %all-to-all-start.1 = ((f32[8,32,128]{2,1,0:T(8,128)}), f32[8,32,128]{2,1,0:T(8,128)S(1)}, u32[]{:S(2)}, u32[]{:S(2)}) async-start(f32[8,32,128]{2,1,0:T(8,128)} %bitcast.204), calls=%async_computation.2 | async-start | bytes 262144 | tf_op jit(solution)/shard_map/all_to_all | solution.py:74
  312.8 261.7 %all-reduce.5.cloned.1.call-start = ((), (), s32[]{:S(2)}) async-start(), calls=%async_computation.5 | async-start | bytes 262144 | tf_op jit(solution)/shard_map/psum | solution.py:14
  313.5 464.1 %reduce-scatter.5.cloned.1.call-start = ((), (), s32[]{:S(2)}) async-start(), calls=%async_computation.7 | async-start | bytes 9437184 | tf_op jit(solution)/shard_map/reduce_scatter | solution.py:78
  332.7 627.0 %reduce-scatter.3.cloned.1.call-start = ((), (), s32[]{:S(2)}) async-start(), calls=%async_computation.6 | async-start | bytes 9437184 | tf_op jit(solution)/shard_map/reduce_scatter | solution.py:78
  602.1 1.3 copy-start.3
  602.1 6.7 copy-start.2
  603.4 8.1 copy-start
  606.9 5.8 copy-start.1
  609.5 3.3 copy-start.5
Sparse Core Ops, SparseCore 0:
  37.7 245.6 all-reduce.2
  316.8 257.6 all-reduce.4
  578.7 198.9 reduce-scatter.4
  781.7 177.9 reduce-scatter.2
where the time goes:
time: 970 us; the launch traced here: 969 us
  waiting for transfers between devices  840 us (87%)
  matrix products  37.4 us (4%)
  between operations  19.3 us (2%)
  other arithmetic  18.8 us (2%)
  local copies, waits for them, and re-layouts  18.7 us (2%)
  blocking collectives  18.5 us (2%)
    psum x2, waiting for transfers between devices, from_root(): return lax.psum(block, axis)  486 us
    reduce_scatter x2, waiting for transfers between devices, block_term(): lax.psum_scatter(partial_value, 'col', scatter_dimension=1, tiled=True)  344 us
  transfers between devices with their start and end apart: 5, of which 5 were waited for; matrix products, arithmetic and copies ran while one was open for 3% of the time, Pallas kernels for 0%

commit v1 on v0

--- a/solution.py
+++ b/solution.py
@@ -11,7 +11,7 @@
 
 def from_root(block, axis, source):
     block = jnp.where(lax.axis_index(axis) == source, block, jnp.zeros_like(block))
-    return lax.psum(block, axis)
+    return jnp.sum(lax.all_gather(block, axis), axis=0)
 
 
 def table_lookup(selected, table):

time: 970 us -> 575 us (0.59)
  waiting for transfers between devices: 840 us -> 437 us
  blocking collectives: 18.5 us -> 39 us
    psum x2 -> x0, waiting for transfers between devices: 486 us -> none  [from_root(): return lax.psum(block, axis)]
    all_gather x0 -> x2, waiting for transfers between devices: none -> 95.8 us  [from_root(): return jnp.sum(lax.all_gather(block, axis), axis=0)]
    all_to_all x1 -> x2, blocking collectives: 18.5 us -> 39 us  [block_term(): lax.all_to_all(solved, 'col', split_axis=0, concat_axis=1, tiled=True)]
    all_to_all x1 -> x0, waiting for transfers between devices: 10.1 us -> none  [block_term(): lax.all_to_all(solved, 'col', split_axis=0, concat_axis=1, tiled=True)]
  transfers between devices with their start and end apart: 5 -> 4, of which waited for: 5 -> 4; matrix products, arithmetic and copies ran while one was open for 3% -> 5% of each run, Pallas kernels for 0% -> 0%
where the time goes in v1:
time: 575 us
  waiting for transfers between devices  437 us (76%)
  blocking collectives  39 us (7%)
  matrix products  34.6 us (6%)
  other arithmetic  23.5 us (4%)
  between operations  19 us (3%)
  local copies, waits for them, and re-layouts  13.6 us (2%)
  loops' own time  8.42 us (1%)
    reduce_scatter x2, waiting for transfers between devices, block_term(): lax.psum_scatter(partial_value, 'col', scatter_dimension=1, tiled=True)  341 us
    all_gather x2, waiting for transfers between devices, from_root(): return jnp.sum(lax.all_gather(block, axis), axis=0)  95.8 us
    all_to_all x2, blocking collectives, block_term(): lax.all_to_all(solved, 'col', split_axis=0, concat_axis=1, tiled=True)  39 us
    dot_general x2, matrix products, block_term(): jnp.dot(basis_cols, matched_rows, precision=exact_mode, preferred_element...  18.1 us
  transfers between devices with their start and end apart: 4, of which 4 were waited for; matrix products, arithmetic and copies ran while one was open for 5% of the time, Pallas kernels for 0%

profile of v1, /device:TPU:34, one launch (start us, length us, event | category | flops | bytes accessed | tf_op | source)
XLA Modules:
  0.0 574.9 jit_solution(7291502497524829737)
XLA Ops:
  7.2 1.3 fusion.233
  12.8 1.7 constant_dynamic-slice_fusion.2
  15.5 2.2 select_reduce_fusion
  17.7 18.8 %while.30 = (s32[]{:T(128)}, f32[256,128]{1,0:T(8,128)S(1)}, f32[256,128]{1,0:T(8,128)S(1)}, f32[256,256]{0,1:T(8,128)S(1)}, f32[128]{0:T(128)S(1)}, /*index=5*/...) while((s32[]{:T(128)}, f32[256,128]{1,0:T(8,128)S(1)}, ...), condition=%wide.region_3.4_spmd, body=%wide.region_2.3_spmd.sunk | while | flops 25882888 | bytes 2812127 | solution.py:69
  38.3 63.1 %all-gather.5.cloned.1.call-done = f32[8192,128]{1,0:T(8,128)} async-done(((f32[256,128]{1,0:T(8,128)}), f32[8192,128]{1,0:T(8,128)}) %all-gather.5.cloned.1.call-update) | async-done | bytes 4194320 | tf_op jit(solution)/shard_map/all_gather | solution.py:14
  101.5 2.4 reduce_sum.38
  105.1 18.8 %while.31 = (s32[]{:T(128)}, f32[256,128]{1,0:T(8,128)S(1)}, f32[256,128]{1,0:T(8,128)S(1)}, f32[256,256]{0,1:T(8,128)S(1)}, f32[128]{0:T(128)S(1)}, /*index=5*/...) while((s32[]{:T(128)}, f32[256,128]{1,0:T(8,128)S(1)}, ...), condition=%wide.region_6.7_spmd, body=%wide.region_5.6_spmd.sunk | while | flops 25882888 | bytes 2812127 | solution.py:69
  123.9 0.7 broadcast_select_fusion
  124.6 19.4 %all_to_all.38 = f32[8,32,128]{2,1,0:T(8,128)S(1)} all-to-all(f32[8,32,128]{2,1,0:T(8,128)S(1)} %bitcast.1119), channel_id=1, replica_groups=mesh['row'=32,'col'=8] {'col'}, dimensions={0} | all-to-all | bytes 262144 | tf_op jit(solution)/shard_map/all_to_all | solution.py:74
  144.0 9.0 %convolution_bitcast_fusion = f32[2048,1024]{0,1:T(8,128)} fusion(f32[2048,2,32]{0,2,1:T(8,128)S(1)} %copy-done.6, f32[8,32,128]{2,1,0:T(8,128)S(1)} %all_to_all.38), kind=kOutput, calls=%fused_computation.342 | convolution fusion | flops 805306368 | bytes 8781824 | tf_op jit(solution)/shard_map/dot_general | solution.py:75
  153.1 32.7 %all-gather.7.cloned.1.call-done = f32[8192,128]{1,0:T(8,128)} async-done(((f32[256,128]{1,0:T(8,128)}), f32[8192,128]{1,0:T(8,128)}) %all-gather.7.cloned.1.call-update) | async-done | bytes 4194320 | tf_op jit(solution)/shard_map/all_gather | solution.py:14
  185.8 2.4 reduce_sum.39
  188.2 19.6 %all_to_all.39 = f32[8,32,128]{2,1,0:T(8,128)S(1)} all-to-all(f32[8,32,128]{2,1,0:T(8,128)S(1)} %bitcast.1124), channel_id=1, replica_groups=mesh['row'=32,'col'=8] {'col'}, dimensions={0} | all-to-all | bytes 262144 | tf_op jit(solution)/shard_map/all_to_all | solution.py:74
  207.8 9.0 %convolution_bitcast_fusion.1 = f32[2048,1024]{0,1:T(8,128)} fusion(f32[2048,2,32]{0,2,1:T(8,128)S(1)} %copy-done.6, f32[8,32,128]{2,1,0:T(8,128)S(1)} %all_to_all.39), kind=kOutput, calls=%fused_computation.343 | convolution fusion | flops 805306368 | bytes 8781824 | tf_op jit(solution)/shard_map/dot_general | solution.py:75
  216.9 0.8 copy.37
  218.5 1.3 fusion.229
  220.2 0.7 copy.49
  221.2 1.2 fusion.217
  222.5 1.3 fusion.207
  223.8 0.8 copy.41
  224.6 158.6 %reduce-scatter.5.cloned.1.call-done = f32[2048,128]{0,1:T(8,128)} async-done(((f32[2048,1024]{0,1:T(8,128)}), f32[2048,128]{0,1:T(8,128)}) %reduce-scatter.5.cloned.1.call-update) | async-done | bytes 1048592 | tf_op jit(solution)/shard_map/reduce_scatter | solution.py:78
  383.2 182.2 %reduce-scatter.3.cloned.1.call-done = f32[2048,128]{0,1:T(8,128)} async-done(((f32[2048,1024]{0,1:T(8,128)}), f32[2048,128]{0,1:T(8,128)}) %reduce-scatter.3.cloned.1.call-update) | async-done | bytes 1048592 | tf_op jit(solution)/shard_map/reduce_scatter | solution.py:78
  565.4 1.7 add_add_fusion
  567.1 1.3 copy.42
  (1172 shorter events, 34.0 us)
Async XLA Ops:
  7.2 94.3 %all-gather.5.cloned.1.call-start = ((), (), s32[]{:S(2)}) async-start(), calls=%async_computation.6 | async-start | bytes 4325376 | tf_op jit(solution)/shard_map/all_gather | solution.py:14
  14.5 1.0 copy-start.3
  14.5 1.0 copy-start.7
  14.5 1.0 copy-start.8
  14.5 1.0 copy-start.9
  37.2 148.6 %all-gather.7.cloned.1.call-start = ((), (), s32[]{:S(2)}) async-start(), calls=%async_computation.7 | async-start | bytes 4325376 | tf_op jit(solution)/shard_map/all_gather | solution.py:14
  105.1 38.9 %copy-start.6 = (f32[2048,2,32]{0,2,1:T(8,128)S(1)}, f32[2048,2,32]{0,2,1:T(8,128)}, u32[]{:S(2)}) copy-start(f32[2048,2,32]{0,2,1:T(8,128)} %param.20) | copy-start | bytes 1572868
  124.6 258.6 %reduce-scatter.5.cloned.1.call-start = ((), (), s32[]{:S(2)}) async-start(), calls=%async_computation.5 | async-start | bytes 9437184 | tf_op jit(solution)/shard_map/reduce_scatter | solution.py:78
  153.1 412.3 %reduce-scatter.3.cloned.1.call-start = ((), (), s32[]{:S(2)}) async-start(), calls=%async_computation.4 | async-start | bytes 9437184 | tf_op jit(solution)/shard_map/reduce_scatter | solution.py:78
  216.9 1.3 copy-start.2
  218.2 3.0 copy-start
  218.5 3.9 copy-start.1
  221.0 1.4 copy-start.4
  221.0 1.4 copy-start.5
Sparse Core Ops, SparseCore 0:
  37.3 64.1 all-gather.4
  124.7 61.0 all-gather.6
  190.0 193.1 reduce-scatter.4
  387.2 178.1 reduce-scatter.2
